TPU v7x, 32 devices: a whole 2x2x4 slice. The times are simulated.
32 devices in a mesh: seq: 8 (over z, x), head: 4 (over y, core).
Axes of the slice: x: 2, y: 2, z: 4, core: 2. Of those that a mesh axis runs over, the one named last changes fastest.
Arguments:
- signal: bfloat16 [4096, 128, 64], P('seq', 'head'), may hold values from -6 to 6
- step_raw: bfloat16 [4096, 128], P('seq', 'head'), may hold values from -3 to 3
- key_proj: bfloat16 [4096, 128], P('seq'), may hold values from -0.69921875 to 0.69921875
- query_proj: bfloat16 [4096, 128], P('seq'), may hold values from -0.69921875 to 0.69921875
- decay_log: float32 [128], P('head'), may hold values from -9 to -3
- skip_gain: float32 [128], P('head'), may hold values from 0.5 to 1.5
- lengths: int32 [6], replicated, may hold values from 1 to 2048, 4096 in all
- cotangent: bfloat16 [4096, 128, 64], P('seq', 'head'), may hold values from -0.59765625 to 0.59765625
Outputs:
- output: bfloat16 [4096, 128, 64], P('seq', 'head')
- grad_signal: bfloat16 [4096, 128, 64], P('seq', 'head')
- grad_keys: bfloat16 [4096, 128], P('seq')
- grad_queries: bfloat16 [4096, 128], P('seq')
Inputs may be any that keep to these rules, and one draw needn't show every extreme that they name: The 6 lengths sum to 4096; the longest is exactly 2048.
All inputs are finite; a program needn't handle non-finite values.
Results may differ from a plain program's by a relative error of at most 0.001.
Values may be sent and summed in bfloat16 or wider, within the bound.
A program may use at most 128 MiB of HBM per device.

v0:
```python
import jax
import jax.numpy as jnp
from jax import lax
from jax.sharding import PartitionSpec as P

SPAN = 256


highest = lax.Precision.HIGHEST


def prefix(part, axis, combine, identity, reverse):
    count = lax.axis_size(axis)
    place = lax.axis_index(axis)
    ahead = count - 1 - place if reverse else place
    gathered = jax.tree.map(lambda a: lax.all_gather(a, axis), part)
    state = jax.tree.map(lambda a, e: jnp.zeros_like(a) + jnp.asarray(e, a.dtype), part, identity)

    def one(step, state):
        source = count - 1 - step if reverse else step
        return combine(
            state, jax.tree.map(lambda a: lax.dynamic_index_in_dim(a, source, 0, False), gathered)
        )

    return lax.fori_loop(0, ahead, one, state)


def span_pass(drive, keys_in, queries_in, logdec, segment, prior_seg, init_state):
    length_all, heads_held, lanes_held = drive.shape
    state_width = keys_in.shape[1]
    blocks_count = length_all // SPAN
    seg_blocks = segment.reshape(blocks_count, SPAN)
    previous = jnp.concatenate([jnp.reshape(prior_seg, (1,)), seg_blocks[:-1, -1]])
    offsets = jnp.arange(SPAN, dtype=jnp.int32)
    causal = offsets[:, None] >= offsets[None, :]
    stacked = (
        drive.reshape(blocks_count, SPAN, heads_held, lanes_held),
        keys_in.reshape(blocks_count, SPAN, state_width),
        queries_in.reshape(blocks_count, SPAN, state_width),
        logdec.reshape(blocks_count, SPAN, heads_held),
        seg_blocks,
        previous,
    )
    state_now = init_state
    block_results = []
    for block_index in range(blocks_count):
        drive_block, keys_block, queries_block, decay_block, seg_block, previous_seg = tuple(
            (member[block_index] for member in stacked)
        )
        local_cum = jnp.cumsum(decay_block, axis=0)
        same_doc = ((seg_block[:, None] == seg_block[None, :]) & causal)[:, :, None]
        log_gap = jnp.where(same_doc, local_cum[:, None, :] - local_cum[None, :, :], 0.0)
        weight = jnp.where(same_doc, jnp.exp(log_gap), 0.0)
        gram_block = jnp.dot(queries_block, keys_block.T, precision=highest)
        within = jnp.einsum(
            "tsh,shp->thp", weight * gram_block[:, :, None], drive_block, precision=highest
        )
        entering = jnp.where((seg_block == previous_seg)[:, None], jnp.exp(local_cum), 0.0)
        carried = (
            jnp.einsum("tn,hpn->thp", queries_block, state_now, precision=highest)
            * entering[:, :, None]
        )
        to_end = jnp.where(
            (seg_block == seg_block[-1])[:, None], jnp.exp(local_cum[-1][None, :] - local_cum), 0.0
        )
        fresh_state = jnp.einsum(
            "sh,sn,shp->hpn", to_end, keys_block, drive_block, precision=highest
        )
        surviving = jnp.where(seg_block[-1] == previous_seg, jnp.exp(local_cum[-1]), 0.0)
        new_state = state_now * surviving[:, None, None] + fresh_state
        state_now = new_state
        result_block = within + carried
        block_results.append(result_block)
    return (jnp.concatenate(block_results, axis=0), state_now)


def link_states(earlier, later):
    return (earlier[0] * later[0], earlier[1] * later[0][:, None, None] + later[1])


def on_device(signal, step_raw, key_proj, query_proj, decay_log, skip_gain, lengths, cotangent):
    tok_dev, heads_loc, width_p = signal.shape
    state_width = key_proj.shape[1]
    doc_ends = jnp.cumsum(lengths)
    start = lax.axis_index("seq") * tok_dev
    places = start + jnp.arange(tok_dev, dtype=jnp.int32)
    segment = jnp.sum((places[:, None] >= doc_ends[None, :]).astype(jnp.int32), axis=1)
    before = jnp.sum((doc_ends <= start - 1).astype(jnp.int32))
    prior_seg = jnp.where(start > 0, before, -1)
    stepsize = jax.nn.softplus(step_raw.astype(jnp.float32))
    logdec = stepsize * (-jnp.exp(decay_log))[None, :]
    signal_f = signal.astype(jnp.float32)
    cotan_f = cotangent.astype(jnp.float32)
    drive = stepsize[:, :, None] * signal_f
    keys_float = key_proj.astype(jnp.float32)
    queries_float = query_proj.astype(jnp.float32)
    zero_state = jnp.zeros((heads_loc, width_p, state_width), jnp.float32)

    def forward(drive_in, keys_in, queries_in):
        return span_pass(drive_in, keys_in, queries_in, logdec, segment, prior_seg, zero_state)

    (scanned, fresh), pullback = jax.vjp(forward, drive, keys_float, queries_float)
    running = jnp.cumsum(logdec, axis=0)
    passing = jnp.where(segment[-1] == prior_seg, jnp.exp(running[-1]), 0.0)
    entering = jnp.where((segment == prior_seg)[:, None], jnp.exp(running), 0.0)
    local_grad = jnp.einsum("th,thp,tn->hpn", entering, cotan_f, queries_float, precision=highest)
    identity = (jnp.ones((heads_loc,), jnp.float32), zero_state)
    incoming = prefix((passing, fresh), "seq", link_states, identity, False)[1]
    later_grad = prefix((passing, local_grad), "seq", link_states, identity, True)[1]
    carried = (
        jnp.einsum("tn,hpn->thp", queries_float, incoming, precision=highest) * entering[:, :, None]
    )
    grad_drive, grad_keys_part, grad_queries_part = pullback((cotan_f, later_grad))
    grad_queries_part = grad_queries_part + jnp.einsum(
        "th,thp,hpn->tn", entering, cotan_f, incoming, precision=highest
    )
    output = (scanned + carried + skip_gain[None, :, None] * signal_f).astype(jnp.bfloat16)
    grad_signal = (grad_drive * stepsize[:, :, None] + skip_gain[None, :, None] * cotan_f).astype(
        jnp.bfloat16
    )
    summed_keys, summed_queries = lax.psum((grad_keys_part, grad_queries_part), "head")
    return (
        output,
        grad_signal,
        summed_keys.astype(jnp.bfloat16),
        summed_queries.astype(jnp.bfloat16),
    )


def solution(mesh):
    in_specs = (
        P("seq", "head", None),
        P("seq", "head"),
        P("seq", None),
        P("seq", None),
        P("head"),
        P("head"),
        P(),
        P("seq", "head", None),
    )
    out_specs = (P("seq", "head", None), P("seq", "head", None), P("seq", None), P("seq", None))
    return jax.shard_map(
        on_device, mesh=mesh, in_specs=in_specs, out_specs=out_specs, check_vma=False
    )
```

profile of v0, /device:TPU:26, one launch (start us, length us, event | category | flops | bytes accessed | tf_op | source)
XLA Modules:
  0.0 355.0 jit_solution(11208577269827473163)
XLA Ops:
  7.2 1.0 reduce-window.29
  8.9 1.4 fusion.155
  10.3 1.2 reduce-window.43
  13.8 4.8 %fusion.36 = f32[32,64,128]{2,1,0:T(8,128)} fusion(bf16[512,32,64]{0,2,1:T(8,128)(2,1)} %param.19, f32[512,32]{0,1:T(8,128)S(1)} %exponential_select_fusion.2, bf16[512,128]{1,0:T(8,128)(2,1)} %param.15), kind=kOutput, calls=%fused_computation.46 | convolution fusion | flops 1612709888 | bytes 3342336 | tf_op jit(solution)/shard_map/th,thp,tn->hpn/dot_general | solution.py:106
  18.7 2.5 dot_general.122
  21.2 0.7 fusion.156
  27.1 16.1 %all-gather.2 = f32[8,1,32]{2,1,0:T(1,128)S(1)} all-gather(f32[1,1,32]{2,1,0:T(1,128)S(1)} %bitcast.207), channel_id=1, replica_groups=mesh['seq'=8,'head'=4] {'seq'}, dimensions={0}, use_global_device_ids=true | all-gather | bytes 1152 | tf_op jit(solution)/shard_map/all_gather | solution.py:16
  44.3 2.0 broadcast_compare_fusion.1
  46.6 0.8 fusion.111
  47.3 0.9 fusion.135
  48.3 0.9 fusion.130
  49.1 92.6 %all-gather.8.cloned.1.call-done = f32[256,64,128]{2,1,0:T(8,128)} async-done(((f32[32,64,128]{2,1,0:T(8,128)}), f32[256,64,128]{2,1,0:T(8,128)}) %all-gather.8.cloned.1.call-update) | async-done | bytes 8388624 | tf_op jit(solution)/shard_map/all_gather | solution.py:16
  142.4 1.0 fusion.119
  143.4 2.7 fusion.69
  146.2 1.0 copy-done.6
  147.2 1.0 fusion.124
  148.3 6.2 %fusion.42 = f32[1,256,32,64]{1,3,2,0:T(8,128)S(1)} fusion(f32[32,64,256]{2,1,0:T(8,128)S(1)} %fusion.119, f32[256,256]{0,1:T(8,128)S(1)} %copy-done.13, f32[256,32]{0,1:T(8,128)S(1)} %copy-done.18, pred[256,256]{0,1:T(8,128)(4,1)S(1)} %copy-done.23, f32[256,32]{0,1:T(8,128)S(1)} %get-tuple-element.162, bf16[512,32,64]{0,2,1:T(8,128)(2,1)S(1)} %copy-done.3), kind=kOutput, calls=%fused_computation.57 | convolution fusion | flops 1620049920 | bytes 5668864 | tf_op jit(solution)/shard_map/transpose(jvp(tsh,shp->thp))/dot_general | solution.py:55
  154.5 6.3 %fusion.41 = f32[1,256,32,64]{1,3,2,0:T(8,128)S(1)} fusion(f32[32,64,256]{2,1,0:T(8,128)S(1)} %fusion.124, f32[256,256]{0,1:T(8,128)S(1)} %copy-done.15, f32[256,32]{0,1:T(8,128)S(1)} %copy-done.21, pred[256,256]{0,1:T(8,128)(4,1)S(1)} %copy-done.25, f32[256,32]{0,1:T(8,128)S(1)} %get-tuple-element.166, bf16[512,32,64]{0,2,1:T(8,128)(2,1)S(1)} %copy-done.3), kind=kOutput, calls=%fused_computation.54 | convolution fusion | flops 1620049920 | bytes 5668864 | tf_op jit(solution)/shard_map/transpose(jvp(tsh,shp->thp))/dot_general | solution.py:55
  161.9 1.0 copy-done.7
  162.9 2.9 add_convert_fusion
  165.8 1.1 fusion.70
  166.9 0.8 copy-done
  167.8 1.0 copy-done.4
  168.7 2.1 fusion.73
  170.9 5.2 %fusion.89 = f32[256,128]{1,0:T(8,128)S(1)} fusion(f32[512,32,64]{0,2,1:T(8,128)} %dot_general.122, f32[256,32]{0,1:T(8,128)S(1)} %get-tuple-element.165), kind=kOutput, calls=%fused_computation.91 | convolution fusion | flops 805830656 | bytes 2260992 | tf_op jit(solution)/shard_map/transpose(jvp(tn,hpn->thp))/dot_general | solution.py:60
  176.1 5.5 %fusion.83 = f32[256,128]{1,0:T(8,128)S(1)} fusion(f32[32,64,128]{2,1,0:T(8,128)} %copy-done.6, f32[512,32,64]{0,2,1:T(8,128)} %copy-done, f32[256,32]{0,1:T(8,128)S(1)} %get-tuple-element.166), kind=kOutput, calls=%fused_computation.89 | convolution fusion | flops 805830656 | bytes 3309568 | tf_op jit(solution)/shard_map/transpose(jvp(sh,sn,shp->hpn))/dot_general | solution.py:66
  181.6 6.4 %fusion = f32[256,256]{0,1:T(8,128)S(1)} fusion(f32[256,32]{0,1:T(8,128)S(1)} %copy-done.22, pred[256,256]{0,1:T(8,128)(4,1)S(1)} %copy-done.26, f32[512,32,64]{0,2,1:T(8,128)S(1)} %copy-done.1, bf16[512,32,64]{0,2,1:T(8,128)(2,1)S(1)} %copy-done.3), kind=kOutput, calls=%fused_computation.5 | convolution fusion | flops 1621032960 | bytes 3538944 | tf_op jit(solution)/shard_map/transpose(jvp(tsh,shp->thp))/dot_general | solution.py:55
  188.2 3.4 fusion.86
  191.7 6.7 %fusion.1 = f32[256,256]{0,1:T(8,128)S(1)} fusion(f32[256,32]{0,1:T(8,128)S(1)} %copy-done.19, pred[256,256]{0,1:T(8,128)(4,1)S(1)} %copy-done.24, f32[512,32,64]{0,2,1:T(8,128)S(1)} %copy-done.1, bf16[512,32,64]{0,2,1:T(8,128)(2,1)S(1)} %copy-done.3), kind=kOutput, calls=%fused_computation.7 | convolution fusion | flops 1621032960 | bytes 3538944 | tf_op jit(solution)/shard_map/transpose(jvp(tsh,shp->thp))/dot_general | solution.py:55
  198.7 0.7 pad_add_fusion.1
  199.9 3.4 fusion.82
  203.7 0.7 pad_add_fusion
  204.5 7.2 %fusion.10 = f32[32,64,256]{2,1,0:T(8,128)S(1)} fusion(f32[256,256]{0,1:T(8,128)S(1)} %copy-done.16, f32[256,32]{0,1:T(8,128)S(1)} %copy-done.22, pred[256,256]{0,1:T(8,128)(4,1)S(1)} %copy-done.26, f32[512,32,64]{0,2,1:T(8,128)S(1)} %copy-done.1), kind=kOutput, calls=%fused_computation.15 | convolution fusion | flops 1619001344 | bytes 4587520 | tf_op jit(solution)/shard_map/jvp(tsh,shp->thp)/dot_general | solution.py:55
  211.6 2.4 fusion.44
  214.0 7.3 %fusion.5 = f32[32,64,256]{2,1,0:T(8,128)S(1)} fusion(f32[256,256]{0,1:T(8,128)S(1)} %copy-done.14, f32[256,32]{0,1:T(8,128)S(1)} %copy-done.19, pred[256,256]{0,1:T(8,128)(4,1)S(1)} %copy-done.24, f32[512,32,64]{0,2,1:T(8,128)S(1)} %copy-done.1), kind=kOutput, calls=%fused_computation.11 | convolution fusion | flops 1619001344 | bytes 4587520 | tf_op jit(solution)/shard_map/jvp(tsh,shp->thp)/dot_general | solution.py:55
  221.3 2.3 fusion.43
  223.7 79.9 %all-gather.6.cloned.1.call-done = f32[256,64,128]{2,1,0:T(8,128)} async-done(((f32[32,64,128]{2,1,0:T(8,128)}), f32[256,64,128]{2,1,0:T(8,128)}) %all-gather.6.cloned.1.call-update) | async-done | bytes 8388624 | tf_op jit(solution)/shard_map/all_gather | solution.py:16
  303.7 10.7 %while.26 = (s32[]{:T(128)}, f32[32,64,128]{2,1,0:T(8,128)S(1)}, s32[]{:T(128)}, f32[8,32]{1,0:T(8,128)S(1)}, f32[8,32,64,128]{3,2,1,0:T(8,128)}, /*index=5*/s32[]{:T(128)}, s32[]{:T(128)}, s32[]{:T(128)}) while((s32[]{:T(128)}, f32[32,64,128]{2,1,0:T(8,128)S(1)}, s32[]{:T(128)}, f32[8,32]{1,0:T(8,128)S(1)}, f32[8,32,64,128]{3,2,1,0:T(8,128)}, ...), condition=%wide.region_10.11_spmd, body=%wide.region_9.10_spmd.sunk | while | flops 524293 | bytes 3146247 | solution.py:25
  303.8 1.5 bitcast_add_fusion.6
  305.3 1.4 bitcast_add_fusion.6
  306.8 1.4 bitcast_add_fusion.6
  308.3 1.4 bitcast_add_fusion.6
  309.8 1.4 bitcast_add_fusion.6
  311.3 1.4 bitcast_add_fusion.6
  312.8 1.4 bitcast_add_fusion.6
  314.4 8.4 %fusion.79 = f32[512,128]{1,0:T(8,128)} fusion(f32[512,128]{1,0:T(8,128)} %bitcast.204, f32[32,64,128]{2,1,0:T(8,128)S(1)} %get-tuple-element.132, bf16[512,32,64]{0,2,1:T(8,128)(2,1)S(1)} %copy-done.3, f32[512,32]{0,1:T(8,128)} %copy-done.11), kind=kOutput, calls=%fused_computation.87 | convolution fusion | flops 1612775424 | bytes 3735552 | tf_op jit(solution)/shard_map/th,thp,hpn->tn/dot_general | solution.py:114
  322.9 18.5 %all-reduce.8 = (bf16[512,128]{1,0:T(8,128)(2,1)}, bf16[512,128]{1,0:T(8,128)(2,1)}) all-reduce(f32[512,128]{1,0:T(8,128)S(1)} %bitcast.203, f32[512,128]{1,0:T(8,128)} %fusion.79), channel_id=1, replica_groups=mesh['seq'=8,'head'=4] {'head'}, use_global_device_ids=true, to_apply=%region_15.16 | all-reduce | flops 131072 | bytes 786432 | tf_op jit(solution)/shard_map/psum | solution.py:121
  341.4 6.5 %fusion.13 = bf16[512,32,64]{0,2,1:T(8,128)(2,1)} fusion(bf16[512,32,64]{0,2,1:T(8,128)(2,1)} %param.12, f32[256,32,64]{0,2,1:T(8,128)} %fusion.43, f32[256,32,64]{0,2,1:T(8,128)} %fusion.44, f32[32,64,128]{2,1,0:T(8,128)S(1)} %get-tuple-element.132, f32[32]{0:T(128)S(1)} %copy-done.27, f32[512,32]{0,1:T(8,128)} %copy-done.11, ...), kind=kOutput, calls=%fused_computation.19 | convolution fusion | flops 1617952768 | bytes 9633920 | tf_op jit(solution)/shard_map/tn,hpn->thp/dot_general | solution.py:111
  (105 shorter events, 9.5 us)
Async XLA Ops:
  7.2 11.5 %copy-start.3 = (bf16[512,32,64]{0,2,1:T(8,128)(2,1)S(1)}, bf16[512,32,64]{0,2,1:T(8,128)(2,1)}, u32[]{:S(2)}) copy-start(bf16[512,32,64]{0,2,1:T(8,128)(2,1)} %param.19) | copy-start | bytes 6291460
  7.2 134.5 %all-gather.8.cloned.1.call-start = ((), (), s32[]{:S(2)}) async-start(), calls=%async_computation.1 | async-start | bytes 9437184 | tf_op jit(solution)/shard_map/all_gather | solution.py:16
  13.2 0.6 copy-start.11
  18.6 28.8 %copy-start.8 = (bf16[512,128]{1,0:T(8,128)(2,1)S(1)}, bf16[512,128]{1,0:T(8,128)(2,1)}, u32[]{:S(2)}) copy-start(bf16[512,128]{1,0:T(8,128)(2,1)} %param.15) | copy-start | bytes 393220
  18.6 28.8 %copy-start.9 = (bf16[512,128]{1,0:T(8,128)(2,1)S(1)}, bf16[512,128]{1,0:T(8,128)(2,1)}, u32[]{:S(2)}) copy-start(bf16[512,128]{1,0:T(8,128)(2,1)} %param.14) | copy-start | bytes 393220
  18.6 285.0 %all-gather.6.cloned.1.call-start = ((), (), s32[]{:S(2)}) async-start(), calls=%async_computation | async-start | bytes 9437184 | tf_op jit(solution)/shard_map/all_gather | solution.py:16
  43.3 0.6 copy-start.20
  44.1 97.6 %copy-start.17 = (f32[256,32]{0,1:T(8,128)}, f32[256,32]{0,1:T(8,128)S(1)}, u32[]{:S(2)}) copy-start(f32[256,32]{0,1:T(8,128)S(1)} %bitcast_bitcast_fusion.1) | copy-start | bytes 98308
  143.4 4.8 %copy-start.13 = (f32[256,256]{0,1:T(8,128)S(1)}, f32[256,256]{0,1:T(8,128)}, u32[]{:S(2)}) copy-start(f32[256,256]{0,1:T(8,128)} %fusion.135) | copy-start | bytes 786436
  143.4 4.8 %copy-start.18 = (f32[256,32]{0,1:T(8,128)S(1)}, f32[256,32]{0,1:T(8,128)}, u32[]{:S(2)}) copy-start(f32[256,32]{0,1:T(8,128)} %copy-done.17) | copy-start | bytes 98308
  143.4 4.8 %copy-start.23 = (pred[256,256]{0,1:T(8,128)(4,1)S(1)}, pred[256,256]{0,1:T(8,128)(4,1)}, u32[]{:S(2)}) copy-start(pred[256,256]{0,1:T(8,128)(4,1)} %get-tuple-element.177) | copy-start | bytes 196612
  146.2 1.0 copy-start.6
  148.2 6.2 %copy-start.15 = (f32[256,256]{0,1:T(8,128)S(1)}, f32[256,256]{0,1:T(8,128)}, u32[]{:S(2)}) copy-start(f32[256,256]{0,1:T(8,128)} %fusion.130) | copy-start | bytes 786436
  148.2 6.2 %copy-start.21 = (f32[256,32]{0,1:T(8,128)S(1)}, f32[256,32]{0,1:T(8,128)}, u32[]{:S(2)}) copy-start(f32[256,32]{0,1:T(8,128)} %copy-done.20) | copy-start | bytes 98308
  148.3 6.2 %copy-start.25 = (pred[256,256]{0,1:T(8,128)(4,1)S(1)}, pred[256,256]{0,1:T(8,128)(4,1)}, u32[]{:S(2)}) copy-start(pred[256,256]{0,1:T(8,128)(4,1)} %get-tuple-element.178) | copy-start | bytes 196612
  161.3 1.6 copy-start.7
  161.3 1.6 copy-start.12
  161.3 1.6 copy-start.27
  165.8 2.0 copy-start
  167.7 1.0 copy-start.4
  170.9 10.7 %copy-start.1 = (f32[512,32,64]{0,2,1:T(8,128)S(1)}, f32[512,32,64]{0,2,1:T(8,128)}, u32[]{:S(2)}) copy-start(f32[512,32,64]{0,2,1:T(8,128)} %copy-done) | copy-start | bytes 12582916
  170.9 10.7 %copy-start.22 = (f32[256,32]{0,1:T(8,128)S(1)}, f32[256,32]{0,1:T(8,128)}, u32[]{:S(2)}) copy-start(f32[256,32]{0,1:T(8,128)} %copy-done.20) | copy-start | bytes 98308
  170.9 10.7 %copy-start.26 = (pred[256,256]{0,1:T(8,128)(4,1)S(1)}, pred[256,256]{0,1:T(8,128)(4,1)}, u32[]{:S(2)}) copy-start(pred[256,256]{0,1:T(8,128)(4,1)} %get-tuple-element.178) | copy-start | bytes 196612
  181.6 10.1 %copy-start.19 = (f32[256,32]{0,1:T(8,128)S(1)}, f32[256,32]{0,1:T(8,128)}, u32[]{:S(2)}) copy-start(f32[256,32]{0,1:T(8,128)} %copy-done.17) | copy-start | bytes 98308
  181.6 10.1 %copy-start.24 = (pred[256,256]{0,1:T(8,128)(4,1)S(1)}, pred[256,256]{0,1:T(8,128)(4,1)}, u32[]{:S(2)}) copy-start(pred[256,256]{0,1:T(8,128)(4,1)} %get-tuple-element.177) | copy-start | bytes 196612
  191.7 8.2 %copy-start.2 = (f32[512,32,64]{0,2,1:T(8,128)S(1)}, f32[512,32,64]{0,2,1:T(8,128)}, u32[]{:S(2)}) copy-start(f32[512,32,64]{0,2,1:T(8,128)} %dot_general.122) | copy-start | bytes 12582916
  191.7 8.2 %copy-start.5 = (f32[32,64,128]{2,1,0:T(8,128)S(1)}, f32[32,64,128]{2,1,0:T(8,128)}, u32[]{:S(2)}) copy-start(f32[32,64,128]{2,1,0:T(8,128)} %copy-done.4) | copy-start | bytes 3145732
  198.5 6.0 %copy-start.16 = (f32[256,256]{0,1:T(8,128)S(1)}, f32[256,256]{0,1:T(8,128)}, u32[]{:S(2)}) copy-start(f32[256,256]{0,1:T(8,128)} %fusion.130) | copy-start | bytes 786436
  211.6 2.4 copy-start.14
  303.7 19.1 %copy-start.10 = (f32[2,256,128]{2,1,0:T(8,128)S(1)}, f32[2,256,128]{2,1,0:T(8,128)}, u32[]{:S(2)}) copy-start(f32[2,256,128]{2,1,0:T(8,128)} %pad_add_fusion.1) | copy-start | bytes 786436
Sparse Core Ops, SparseCore 0:
  18.7 122.9 all-gather.7
  171.0 132.5 all-gather.5
where the time goes:
time: 359 us; the launch traced here: 355 us
  waiting for transfers between devices  173 us (48%)
  matrix products  93.1 us (26%)
  blocking collectives  34.6 us (10%)
  other arithmetic  27.2 us (8%)
  between operations  18.2 us (5%)
  local copies, waits for them, and re-layouts  8.2 us (2%)
    all_gather x2, waiting for transfers between devices, prefix(): gathered = jax.tree.map(lambda a: lax.all_gather(a, axis), part)  173 us
    dot_general x6, matrix products, span_pass(): jnp.einsum('tsh,shp->thp', weight * gram_block[:, :, None], drive_block,...  40.1 us
    psum x1, blocking collectives, on_device(): lax.psum((grad_keys_part, grad_queries_part), 'head')  18.5 us
    all_gather x1, blocking collectives, prefix(): gathered = jax.tree.map(lambda a: lax.all_gather(a, axis), part)  16.1 us
    dot_general x5, matrix products, span_pass(): jnp.einsum('tn,hpn->thp', queries_block, state_now, precision=highest)  16.1 us
    dot_general x6, matrix products, span_pass(): jnp.einsum('sh,sn,shp->hpn', to_end, keys_block, drive_block, precision=h...  14.2 us
    add x7, other arithmetic, link_states(): earlier[1] * later[0][:, None, None] + later[1]  10.2 us
    dot_general x1, matrix products, on_device(): jnp.einsum('th,thp,hpn->tn', entering, cotan_f, incoming, precision=highest)  8.42 us
  transfers between devices with their start and end apart: 2, of which 2 were waited for; matrix products, arithmetic and copies ran while one was open for 18% of the time, Pallas kernels for 0%

commit v1 on v0

v1 whole, which is shorter than its diff:
```python
import functools

import jax
import jax.numpy as jnp
from jax import lax
from jax.experimental import pallas as pl
from jax.experimental.pallas import tpu as pltpu
from jax.sharding import PartitionSpec as P

MESH = pl.DeviceIdType.MESH
F32 = jnp.float32
BF16 = jnp.bfloat16
GROUP = 4


def mm(a, b, ca=1, cb=0):
    return lax.dot_general(a, b, (((ca,), (cb,)), ((), ())), preferred_element_type=F32)


def split(a):
    hi = a.astype(BF16)
    return hi, (a - hi.astype(F32)).astype(BF16)


def mm3(a, b, ca=1, cb=0):
    return mm(a[0], b[0], ca, cb) + mm(a[0], b[1], ca, cb) + mm(a[1], b[0], ca, cb)


def kernel(
    nseq, nhead, len_ref, sig, cot, step_ref, key_ref, query_ref, dl_ref, sk_ref,
    out_ref, gs_ref, gk_ref, gq_ref,
    bh, bl, ah, al, ys, zs, macc, gh, gl, gth, gtl, km, qm, e3, f3, pass3, ss3, sd3, sk3,
    sl, dlo, passr, r1s, r1d, zss, zds, zsr, zdr, rts, rtd, ins, ind, gg, rb, agb, gacc,
    psem, xsem, zsem, tsem, hsem, asem,
):
    heads, width, tok = sig.shape
    state = key_ref.shape[1]
    blocks = 2 * GROUP
    hb = heads // blocks
    rows = hb * width
    half = tok // 2
    me, hd = lax.axis_index("seq"), lax.axis_index("head")
    x, z = lax.rem(me, 2), me // 2
    nz = nseq // 2
    partner = me + 1 - 2 * x
    first, last = z == 0, z == nz - 1

    barrier = pltpu.get_barrier_semaphore()

    def greet(seq, head):
        pl.semaphore_signal(barrier, inc=1, device_id=(seq, head), device_id_type=MESH)

    greet(partner, hd)

    @pl.when(z > 0)
    def _():
        greet(me - 2, hd)

    @pl.when(z < nz - 1)
    def _():
        greet(me + 2, hd)

    for d in range(1, nhead):
        greet(me, lax.rem(hd + d, nhead))
    pl.semaphore_wait(barrier, nhead + jnp.where(first, 0, 1) + jnp.where(last, 0, 1))

    def hblock(b):
        return pl.ds(b * hb, hb)

    def rcopy(src, dst, sems, index, seq, head=None):
        return pltpu.make_async_remote_copy(
            src_ref=src, dst_ref=dst, send_sem=sems.at[(0,) + index], recv_sem=sems.at[(1,) + index],
            device_id=(seq, hd if head is None else head), device_id_type=MESH,
        )

    start = me * tok
    end, ends = jnp.int32(0), []
    for k in range(len_ref.shape[0]):
        end = end + len_ref[k]
        ends.append(end)

    def segment(places):
        total = jnp.zeros_like(places)
        for value in ends:
            total = total + jnp.where(places >= value, 1, 0)
        return total

    seg_last = segment(start + tok - 1)
    prior = jnp.where(start > 0, segment(start - 1), -1)
    seg_col = segment(start + lax.broadcasted_iota(jnp.int32, (tok, 1), 0))
    seg_row = segment(start + lax.broadcasted_iota(jnp.int32, (1, tok), 1))
    r_id = lax.broadcasted_iota(jnp.int32, (tok, tok), 0)
    c_id = lax.broadcasted_iota(jnp.int32, (tok, tok), 1)
    upper = jnp.where(r_id <= c_id, 1.0, 0.0).astype(BF16)

    raw = step_ref[...].astype(F32)
    size = jnp.maximum(raw, 0.0) + jnp.log1p(jnp.exp(-jnp.abs(raw)))
    logdec = size * (-jnp.exp(dl_ref[:, 0:1]))
    one = logdec.astype(BF16)
    rest = logdec - one.astype(F32)
    two, three = split(rest)
    cum = mm(three, upper) + mm(two, upper) + mm(one, upper)
    mid, final = cum[:, half - 1 : half], cum[:, tok - 1 : tok]
    e = jnp.exp(cum - mid)
    f = size * jnp.exp(mid - cum)
    lanes = (heads, state)
    passing = jnp.broadcast_to(jnp.where(seg_last == prior, jnp.exp(final), 0.0), lanes)
    to_last = jnp.broadcast_to(jnp.exp(final - mid), lanes)
    to_mid = jnp.broadcast_to(jnp.exp(mid), lanes)
    for b in range(blocks):
        part = slice(b * hb, (b + 1) * hb)
        e3[b], f3[b] = e[part], f[part]
        pass3[b], ss3[b], sd3[b] = passing[part], to_last[part], to_mid[part]
        sk3[b] = sk_ref[part, :]

    rcopy(pass3, passr, psem, (), partner).start()

    keys, queries = key_ref[...], query_ref[...]
    km[...] = jnp.where(seg_col == seg_last, keys.astype(F32), 0.0).astype(BF16)
    qm[...] = jnp.where(seg_col == prior, queries.astype(F32), 0.0).astype(BF16)

    def p1(b):
        bf = sig[hblock(b)].astype(F32) * f3[b][:, None, :]
        hi, lo = split(bf.reshape(rows, tok))
        bh[b], bl[b] = hi, lo
        kk = km[...]
        sl[b] = (mm(hi, kk) + mm(lo, kk)).reshape(hb, width, state) * ss3[b][:, None, :]
        af = cot[hblock(b)].astype(F32) * e3[b][:, None, :]
        hi, lo = split(af.reshape(rows, tok))
        ah[b], al[b] = hi, lo
        qq = qm[...]
        dlo[b] = (mm(hi, qq) + mm(lo, qq)).reshape(hb, width, state) * sd3[b][:, None, :]

    def x_copy(k):
        b = (1 - x) * GROUP + k
        return (
            rcopy(sl.at[b], r1s.at[k], xsem, (0, k), partner),
            rcopy(dlo.at[b], r1d.at[k], xsem, (1, k), partner),
        )

    @pl.loop(0, GROUP)
    def _(k):
        p1((1 - x) * GROUP + k)
        for copy in x_copy(k):
            copy.start()

    @pl.loop(0, GROUP)
    def _(k):
        p1(x * GROUP + k)

    same = seg_col == seg_row
    gram = jnp.where(same & (r_id >= c_id), mm(queries, keys, 1, 1), 0.0)
    gh[...], gl[...] = split(gram)
    gram_t = jnp.where(same & (r_id <= c_id), mm(keys, queries, 1, 1), 0.0)
    gth[...], gtl[...] = split(gram_t)
    macc[...] = jnp.zeros_like(macc)
    gacc[...] = jnp.zeros_like(gacc)

    def p2(b):
        bb = (bh[b], bl[b])
        aa = (ah[b], al[b])
        b0 = (bb[0][:, :half], bb[1][:, :half])
        a0 = (aa[0][:, :half], aa[1][:, :half])
        a1 = (aa[0][:, half:], aa[1][:, half:])
        ys[b, :, :half] = mm3(b0, (gth[:half, :half], gtl[:half, :half]))
        ys[b, :, half:] = mm3(bb, (gth[:, half:], gtl[:, half:]))
        zs[b, :, half:] = mm3(a1, (gh[half:, half:], gl[half:, half:]))
        zs[b, :, :half] = mm3(aa, (gh[:, :half], gl[:, :half]))
        macc[:half, :half] += mm3(a0, b0, 0, 0)
        macc[half:, :] += mm3(a1, bb, 0, 0)

    def z_copy(k):
        return (
            rcopy(zss.at[k], zsr.at[k], zsem, (0, k), me + 2),
            rcopy(zds.at[k], zdr.at[k], zsem, (1, k), me - 2),
        )

    def t_copy(k, mine):
        b = jnp.where(mine, x, 1 - x) * GROUP + k
        return (
            rcopy(rts.at[k], ins.at[b], tsem, (0, k), partner),
            rcopy(rtd.at[k], ind.at[b], tsem, (1, k), partner),
        )

    rcopy(pass3, passr, psem, (), partner).wait_recv()

    @pl.loop(0, GROUP)
    def _(k):
        p2(2 * k)
        b = x * GROUP + k
        for copy in x_copy(k):
            copy.wait_recv()
        left = x == 0
        own, other = pass3[b][:, None, :], passr[b][:, None, :]
        pass0, pass1 = jnp.where(left, own, other), jnp.where(left, other, own)
        s0, s1 = jnp.where(left, sl[b], r1s[k]), jnp.where(left, r1s[k], sl[b])
        d0, d1 = jnp.where(left, dlo[b], r1d[k]), jnp.where(left, r1d[k], dlo[b])
        both = pass0 * pass1
        ps, pd = pass1 * s0 + s1, d0 + pass0 * d1
        to_next, to_prev = z_copy(k)

        @pl.when(first)
        def _():
            zsr[k] = jnp.zeros_like(ps)

        @pl.when(first & (nz > 1))
        def _():
            zss[k] = ps
            to_next.start()

        @pl.when(last)
        def _():
            zdr[k] = jnp.zeros_like(pd)

        @pl.when(last & (nz > 1))
        def _():
            zds[k] = pd
            to_prev.start()

        p2(2 * k + 1)

        @pl.when(z > 0)
        def _():
            to_next.wait_recv()

        @pl.when((z > 0) & (z < nz - 1))
        def _():
            zss[k] = both * zsr[k] + ps
            to_next.start()

        @pl.when(z < nz - 1)
        def _():
            to_prev.wait_recv()

        @pl.when((z > 0) & (z < nz - 1))
        def _():
            zds[k] = both * zdr[k] + pd
            to_prev.start()

        in0 = zsr[k]
        in1 = pass0 * in0 + s0
        gin1 = zdr[k]
        gin0 = pass1 * gin1 + d1
        rts[k] = jnp.where(left, in1, in0)
        rtd[k] = jnp.where(left, gin1, gin0)
        for copy in t_copy(k, True):
            copy.start()
        ins[b] = jnp.where(left, in0, in1)
        ind[b] = jnp.where(left, gin0, gin1)

    mixed = split(jnp.where(same & (r_id >= c_id), macc[...], 0.0))
    gq_local = mm(mixed[0], keys) + mm(mixed[1], keys)
    gk_local = mm(mixed[0], queries, 0, 0) + mm(mixed[1], queries, 0, 0)

    def p3(b):
        s = split((ins[b] * sd3[b][:, None, :]).reshape(rows, state))
        d = split((ind[b] * ss3[b][:, None, :]).reshape(rows, state))
        qq, kk = qm[...], km[...]
        y = ys[b] + mm(s[0], qq, 1, 1) + mm(s[1], qq, 1, 1)
        zz = zs[b] + mm(d[0], kk, 1, 1) + mm(d[1], kk, 1, 1)
        skip = sk3[b][:, 0:1][:, :, None]
        shape = (hb, width, tok)
        out_ref[hblock(b)] = (
            y.reshape(shape) * e3[b][:, None, :] + skip * sig[hblock(b)].astype(F32)
        ).astype(BF16)
        gs_ref[hblock(b)] = (
            zz.reshape(shape) * f3[b][:, None, :] + skip * cot[hblock(b)].astype(F32)
        ).astype(BF16)
        gacc[:, :state] += mm3((bh[b], bl[b]), d, 0, 0)
        gacc[:, state:] += mm3((ah[b], al[b]), s, 0, 0)

    @pl.loop(0, GROUP)
    def _(k):
        p3(x * GROUP + k)

    @pl.loop(0, GROUP)
    def _(k):
        for copy in t_copy(k, False):
            copy.wait_recv()
        p3((1 - x) * GROUP + k)

    piece = tok // nhead
    gk = gk_local + jnp.where(seg_col == seg_last, gacc[:, :state], 0.0)
    gq = gq_local + jnp.where(seg_col == prior, gacc[:, state:], 0.0)
    for j in range(nhead):
        part = slice(j * piece, (j + 1) * piece)
        gg[j, :, :state] = gk[part]
        gg[j, :, state:] = gq[part]

    def h_copy(d):
        to = lax.rem(hd + d, nhead)
        return rcopy(gg.at[to], rb.at[d], hsem, (d,), me, to)

    def a_copy(d, sender):
        to = lax.rem(hd + d, nhead)
        return rcopy(agb.at[sender], agb.at[sender], asem, (d,), me, to)

    for d in range(1, nhead):
        h_copy(d).start()
    total = gg[hd]
    for d in range(1, nhead):
        h_copy(d).wait_recv()
        total = total + rb[d]
    agb[hd] = total.astype(BF16)
    for d in range(1, nhead):
        a_copy(d, hd).start()
    for d in range(1, nhead):
        a_copy(d, lax.rem(hd + nhead - d, nhead)).wait_recv()
    for j in range(nhead):
        part = slice(j * piece, (j + 1) * piece)
        gk_ref[part, :] = agb[j, :, :state]
        gq_ref[part, :] = agb[j, :, state:]

    for d in range(1, nhead):
        h_copy(d).wait_send()
        a_copy(d, hd).wait_send()
    rcopy(pass3, passr, psem, (), partner).wait_send()

    @pl.loop(0, GROUP)
    def _(k):
        for copy in x_copy(k) + t_copy(k, True):
            copy.wait_send()
        to_next, to_prev = z_copy(k)

        @pl.when(z < nz - 1)
        def _():
            to_next.wait_send()

        @pl.when(z > 0)
        def _():
            to_prev.wait_send()


def solution(mesh):
    nseq, nhead = mesh.shape["seq"], mesh.shape["head"]

    def on_device(signal, step_raw, key_proj, query_proj, decay_log, skip_gain, lengths, cotangent):
        tok, heads, width = signal.shape
        state = key_proj.shape[1]
        blocks = 2 * GROUP
        hb = heads // blocks
        rows = hb * width
        piece = tok // nhead
        dma = pltpu.SemaphoreType.DMA
        vmem = pltpu.VMEM
        st = (hb, width, state)
        scratch = (
            [vmem((blocks, rows, tok), BF16)] * 4
            + [vmem((blocks, rows, tok), F32)] * 2
            + [vmem((tok, tok), F32)]
            + [vmem((tok, tok), BF16)] * 4
            + [vmem((tok, state), BF16)] * 2
            + [vmem((blocks, hb, tok), F32)] * 2
            + [vmem((blocks, hb, state), F32)] * 4
            + [vmem((blocks,) + st, F32)] * 2
            + [vmem((blocks, hb, state), F32)]
            + [vmem((GROUP,) + st, F32)] * 8
            + [vmem((blocks,) + st, F32)] * 2
            + [vmem((nhead, piece, 2 * state), F32)] * 2
            + [vmem((nhead, piece, 2 * state), BF16)]
            + [vmem((tok, 2 * state), F32)]
            + [dma((2,))]
            + [dma((2, 2, GROUP))] * 3
            + [dma((2, nhead))] * 2
        )
        turned = jax.ShapeDtypeStruct((heads, width, tok), BF16)
        grads = jax.ShapeDtypeStruct((tok, state), BF16)
        whole = pl.BlockSpec(memory_space=pltpu.VMEM)
        out, gs, gk, gq = pl.pallas_call(
            functools.partial(kernel, nseq, nhead),
            out_shape=(turned, turned, grads, grads),
            in_specs=[pl.BlockSpec(memory_space=pltpu.SMEM)] + [whole] * 7,
            out_specs=(whole,) * 4,
            scratch_shapes=scratch,
            compiler_params=pltpu.CompilerParams(
                collective_id=0, has_side_effects=True, vmem_limit_bytes=60 << 20
            ),
        )(
            lengths,
            jnp.transpose(signal, (1, 2, 0)),
            jnp.transpose(cotangent, (1, 2, 0)),
            step_raw.T,
            key_proj,
            query_proj,
            jnp.broadcast_to(decay_log[:, None], (heads, state)),
            jnp.broadcast_to(skip_gain[:, None], (heads, state)),
        )
        return jnp.transpose(out, (2, 0, 1)), jnp.transpose(gs, (2, 0, 1)), gk, gq

    in_specs = (
        P("seq", "head", None),
        P("seq", "head"),
        P("seq", None),
        P("seq", None),
        P("head"),
        P("head"),
        P(),
        P("seq", "head", None),
    )
    out_specs = (P("seq", "head", None), P("seq", "head", None), P("seq", None), P("seq", None))
    return jax.shard_map(
        on_device, mesh=mesh, in_specs=in_specs, out_specs=out_specs, check_vma=False
    )
```

time: 359 us -> 112 us (0.31)
  the two profiles are of different devices: /device:TPU:26 before, /device:TPU:1 now
where the time goes in v1:
time: 112 us
  Pallas kernels  103 us (92%)
  local copies, waits for them, and re-layouts  8.58 us (8%)
    pallas_call x1, Pallas kernels, on_device(): pl.pallas_call(functools.partial(kernel, nseq, nhead), out_shape=(turned,...  103 us
    unnamed x10, local copies, waits for them, and re-layouts  5.92 us

profile of v1, /device:TPU:1, one launch (start us, length us, event | category | flops | bytes accessed | tf_op | source)
XLA Modules:
  0.0 112.2 jit_solution(11566829737833314014)
XLA Ops:
  0.6 1.3 %broadcast_in_dim.4.dl_ref = f32[32,128]{1,0:T(8,128)} broadcast(f32[32]{0:T(128)} %param.12), dimensions={0} | broadcast | bytes 16512 | tf_op jit(solution)/shard_map/broadcast_in_dim | solution.py:385
  2.0 1.3 %broadcast_in_dim.5.sk_ref = f32[32,128]{1,0:T(8,128)} broadcast(f32[32]{0:T(128)} %param.13), dimensions={0} | broadcast | bytes 16512 | tf_op jit(solution)/shard_map/broadcast_in_dim | solution.py:386
  3.3 102.9 %shard_map.111 = (bf16[32,64,512]{2,1,0:T(8,128)(2,1)}, bf16[32,64,512]{2,1,0:T(8,128)(2,1)}, bf16[512,128]{1,0:T(8,128)(2,1)}, bf16[512,128]{1,0:T(8,128)(2,1)}) custom-call(s32[6]{0:T(128)} %len_ref.1, bf16[32,64,512]{2,1,0:T(8,128)(2,1)} %bitcast.5, bf16[32,64,512]{2,1,0:T(8,128)(2,1)} %bitcast.6, bf16[32,512]{1,0:T(8,128)(2,1)} %bitcast.9, ...), custom_call_target="tpu_custom_call" | custom-call | tf_op jit(solution)/shard_map/pallas_call | solution.py:369
  106.2 0.0 copy-start
  106.3 3.3 %copy.16 = bf16[512,32,64]{0,2,1:T(8,128)(2,1)} copy(bf16[512,32,64]{0,2,1:T(8,128)(2,1)} %bitcast.8) | data formatting | bytes 4194304
  109.5 0.0 copy-done
  109.5 0.0 copy-start.2
  109.5 0.0 copy-start.1
  109.5 1.3 %copy.17 = bf16[512,32,64]{0,2,1:T(8,128)(2,1)} copy(bf16[512,32,64]{0,2,1:T(8,128)(2,1)S(1)} %bitcast.7) | data formatting | bytes 4194304
  110.9 0.0 copy-done.2
  110.9 0.7 copy.18
  111.5 0.0 copy-done.1
  111.5 0.7 copy.19
Async XLA Ops:
  106.2 3.3 %copy-start = (bf16[32,64,512]{2,1,0:T(8,128)(2,1)S(1)}, bf16[32,64,512]{2,1,0:T(8,128)(2,1)}, u32[]{:S(2)}) copy-start(bf16[32,64,512]{2,1,0:T(8,128)(2,1)} %get-tuple-element.9) | copy-start | bytes 6291460
  109.5 1.3 %copy-start.2 = (bf16[512,128]{1,0:T(8,128)(2,1)S(1)}, bf16[512,128]{1,0:T(8,128)(2,1)}, u32[]{:S(2)}) copy-start(bf16[512,128]{1,0:T(8,128)(2,1)} %get-tuple-element.18) | copy-start | bytes 393220
  109.5 2.0 %copy-start.1 = (bf16[512,128]{1,0:T(8,128)(2,1)S(1)}, bf16[512,128]{1,0:T(8,128)(2,1)}, u32[]{:S(2)}) copy-start(bf16[512,128]{1,0:T(8,128)(2,1)} %get-tuple-element.19) | copy-start | bytes 393220

commit v2 on v1

--- a/solution.py
+++ b/solution.py
@@ -26,12 +26,22 @@
     return mm(a[0], b[0], ca, cb) + mm(a[0], b[1], ca, cb) + mm(a[1], b[0], ca, cb)
 
 
+def quant(v, axis):
+    top = jnp.maximum(jnp.max(jnp.abs(v), axis=axis, keepdims=True), 1e-30)
+    code = jnp.round(v * (32000.0 / top)).astype(jnp.int32).astype(jnp.int16)
+    return code, top * (1.0 / 32000.0)
+
+
+def wide(code, scale):
+    return code.astype(jnp.int32).astype(F32) * scale
+
+
 def kernel(
     nseq, nhead, len_ref, sig, cot, step_ref, key_ref, query_ref, dl_ref, sk_ref,
     out_ref, gs_ref, gk_ref, gq_ref,
     bh, bl, ah, al, ys, zs, macc, gh, gl, gth, gtl, km, qm, e3, f3, pass3, ss3, sd3, sk3,
-    sl, dlo, passr, r1s, r1d, zss, zds, zsr, zdr, rts, rtd, ins, ind, gg, rb, agb, gacc,
-    psem, xsem, zsem, tsem, hsem, asem,
+    sl, dlo, zsr, zdr, ins, ind, xq, xqr, tq, tqr, xs, xsr, zq, zqr, zc, zcr, ts, tsr,
+    gg, hq, hqr, hs, hsr, agb, gacc, xsem, zsem, tsem, hsem, asem,
 ):
     heads, width, tok = sig.shape
     state = key_ref.shape[1]
@@ -95,7 +105,11 @@
 
     raw = step_ref[...].astype(F32)
     size = jnp.maximum(raw, 0.0) + jnp.log1p(jnp.exp(-jnp.abs(raw)))
-    logdec = size * (-jnp.exp(dl_ref[:, 0:1]))
+    eye = lax.broadcasted_iota(jnp.int32, (heads, heads), 0) == lax.broadcasted_iota(
+        jnp.int32, (heads, heads), 1
+    )
+    column = lambda ref: jnp.sum(jnp.where(eye, ref[...], 0.0), axis=1, keepdims=True)
+    logdec = size * (-jnp.exp(column(dl_ref)))
     one = logdec.astype(BF16)
     rest = logdec - one.astype(F32)
     two, three = split(rest)
@@ -107,13 +121,12 @@
     passing = jnp.broadcast_to(jnp.where(seg_last == prior, jnp.exp(final), 0.0), lanes)
     to_last = jnp.broadcast_to(jnp.exp(final - mid), lanes)
     to_mid = jnp.broadcast_to(jnp.exp(mid), lanes)
+    skips = jnp.broadcast_to(column(sk_ref), lanes)
     for b in range(blocks):
         part = slice(b * hb, (b + 1) * hb)
         e3[b], f3[b] = e[part], f[part]
         pass3[b], ss3[b], sd3[b] = passing[part], to_last[part], to_mid[part]
-        sk3[b] = sk_ref[part, :]
-
-    rcopy(pass3, passr, psem, (), partner).start()
+        sk3[b] = skips[part]
 
     keys, queries = key_ref[...], query_ref[...]
     km[...] = jnp.where(seg_col == seg_last, keys.astype(F32), 0.0).astype(BF16)
@@ -132,15 +145,20 @@
         dlo[b] = (mm(hi, qq) + mm(lo, qq)).reshape(hb, width, state) * sd3[b][:, None, :]
 
     def x_copy(k):
+        return (
+            rcopy(xq.at[k], xqr.at[k], xsem, (0, k), partner),
+            rcopy(xs.at[k], xsr.at[k], xsem, (1, k), partner),
+        )
+
+    @pl.loop(0, GROUP)
+    def _(k):
         b = (1 - x) * GROUP + k
-        return (
-            rcopy(sl.at[b], r1s.at[k], xsem, (0, k), partner),
-            rcopy(dlo.at[b], r1d.at[k], xsem, (1, k), partner),
-        )
-
-    @pl.loop(0, GROUP)
-    def _(k):
-        p1((1 - x) * GROUP + k)
+        p1(b)
+        code, scale = quant(sl[b], 1)
+        xq[k, 0], xs[k, 0] = code, scale[:, 0, :]
+        code, scale = quant(dlo[b], 1)
+        xq[k, 1], xs[k, 1] = code, scale[:, 0, :]
+        xs[k, 2] = pass3[b]
         for copy in x_copy(k):
             copy.start()
 
@@ -171,18 +189,32 @@
 
     def z_copy(k):
         return (
-            rcopy(zss.at[k], zsr.at[k], zsem, (0, k), me + 2),
-            rcopy(zds.at[k], zdr.at[k], zsem, (1, k), me - 2),
-        )
-
-    def t_copy(k, mine):
-        b = jnp.where(mine, x, 1 - x) * GROUP + k
+            (
+                rcopy(zq.at[0, k], zqr.at[0, k], zsem, (0, 0, k), me + 2),
+                rcopy(zc.at[0, k], zcr.at[0, k], zsem, (0, 1, k), me + 2),
+            ),
+            (
+                rcopy(zq.at[1, k], zqr.at[1, k], zsem, (1, 0, k), me - 2),
+                rcopy(zc.at[1, k], zcr.at[1, k], zsem, (1, 1, k), me - 2),
+            ),
+        )
+
+    def t_copy(k):
         return (
-            rcopy(rts.at[k], ins.at[b], tsem, (0, k), partner),
-            rcopy(rtd.at[k], ind.at[b], tsem, (1, k), partner),
-        )
-
-    rcopy(pass3, passr, psem, (), partner).wait_recv()
+            rcopy(tq.at[k], tqr.at[k], tsem, (0, k), partner),
+            rcopy(ts.at[k], tsr.at[k], tsem, (1, k), partner),
+        )
+
+    def z_send(way, k, value, copies):
+        code, scale = quant(value, 1)
+        zq[way, k], zc[way, k] = code, scale[:, 0, :]
+        for copy in copies:
+            copy.start()
+
+    def z_take(way, k, into, copies):
+        for copy in copies:
+            copy.wait_recv()
+        into[k] = wide(zqr[way, k], zcr[way, k][:, None, :])
 
     @pl.loop(0, GROUP)
     def _(k):
@@ -191,10 +223,12 @@
         for copy in x_copy(k):
             copy.wait_recv()
         left = x == 0
-        own, other = pass3[b][:, None, :], passr[b][:, None, :]
+        own, other = pass3[b][:, None, :], xsr[k, 2][:, None, :]
+        s_in = wide(xqr[k, 0], xsr[k, 0][:, None, :])
+        d_in = wide(xqr[k, 1], xsr[k, 1][:, None, :])
         pass0, pass1 = jnp.where(left, own, other), jnp.where(left, other, own)
-        s0, s1 = jnp.where(left, sl[b], r1s[k]), jnp.where(left, r1s[k], sl[b])
-        d0, d1 = jnp.where(left, dlo[b], r1d[k]), jnp.where(left, r1d[k], dlo[b])
+        s0, s1 = jnp.where(left, sl[b], s_in), jnp.where(left, s_in, sl[b])
+        d0, d1 = jnp.where(left, dlo[b], d_in), jnp.where(left, d_in, dlo[b])
         both = pass0 * pass1
         ps, pd = pass1 * s0 + s1, d0 + pass0 * d1
         to_next, to_prev = z_copy(k)
@@ -205,8 +239,7 @@
 
         @pl.when(first & (nz > 1))
         def _():
-            zss[k] = ps
-            to_next.start()
+            z_send(0, k, ps, to_next)
 
         @pl.when(last)
         def _():
@@ -214,36 +247,35 @@
 
         @pl.when(last & (nz > 1))
         def _():
-            zds[k] = pd
-            to_prev.start()
+            z_send(1, k, pd, to_prev)
 
         p2(2 * k + 1)
 
         @pl.when(z > 0)
         def _():
-            to_next.wait_recv()
+            z_take(0, k, zsr, to_next)
 
         @pl.when((z > 0) & (z < nz - 1))
         def _():
-            zss[k] = both * zsr[k] + ps
-            to_next.start()
+            z_send(0, k, both * zsr[k] + ps, to_next)
 
         @pl.when(z < nz - 1)
         def _():
-            to_prev.wait_recv()
+            z_take(1, k, zdr, to_prev)
 
         @pl.when((z > 0) & (z < nz - 1))
         def _():
-            zds[k] = both * zdr[k] + pd
-            to_prev.start()
+            z_send(1, k, both * zdr[k] + pd, to_prev)
 
         in0 = zsr[k]
         in1 = pass0 * in0 + s0
         gin1 = zdr[k]
         gin0 = pass1 * gin1 + d1
-        rts[k] = jnp.where(left, in1, in0)
-        rtd[k] = jnp.where(left, gin1, gin0)
-        for copy in t_copy(k, True):
+        code, scale = quant(jnp.where(left, in1, in0), 1)
+        tq[k, 0], ts[k, 0] = code, scale[:, 0, :]
+        code, scale = quant(jnp.where(left, gin1, gin0), 1)
+        tq[k, 1], ts[k, 1] = code, scale[:, 0, :]
+        for copy in t_copy(k):
             copy.start()
         ins[b] = jnp.where(left, in0, in1)
         ind[b] = jnp.where(left, gin0, gin1)
@@ -275,9 +307,12 @@
 
     @pl.loop(0, GROUP)
     def _(k):
-        for copy in t_copy(k, False):
+        for copy in t_copy(k):
             copy.wait_recv()
-        p3((1 - x) * GROUP + k)
+        b = (1 - x) * GROUP + k
+        ins[b] = wide(tqr[k, 0], tsr[k, 0][:, None, :])
+        ind[b] = wide(tqr[k, 1], tsr[k, 1][:, None, :])
+        p3(b)
 
     piece = tok // nhead
     gk = gk_local + jnp.where(seg_col == seg_last, gacc[:, :state], 0.0)
@@ -289,18 +324,26 @@
 
     def h_copy(d):
         to = lax.rem(hd + d, nhead)
-        return rcopy(gg.at[to], rb.at[d], hsem, (d,), me, to)
+        return (
+            rcopy(hq.at[to], hqr.at[d], hsem, (0, d), me, to),
+            rcopy(hs.at[to], hsr.at[d], hsem, (1, d), me, to),
+        )
 
     def a_copy(d, sender):
         to = lax.rem(hd + d, nhead)
         return rcopy(agb.at[sender], agb.at[sender], asem, (d,), me, to)
 
     for d in range(1, nhead):
-        h_copy(d).start()
+        to = lax.rem(hd + d, nhead)
+        code, scale = quant(gg[to], 0)
+        hq[to], hs[to] = code, jnp.broadcast_to(scale, hs.shape[1:])
+        for copy in h_copy(d):
+            copy.start()
     total = gg[hd]
     for d in range(1, nhead):
-        h_copy(d).wait_recv()
-        total = total + rb[d]
+        for copy in h_copy(d):
+            copy.wait_recv()
+        total = total + wide(hqr[d], hsr[d][0:1, :])
     agb[hd] = total.astype(BF16)
     for d in range(1, nhead):
         a_copy(d, hd).start()
@@ -312,23 +355,25 @@
         gq_ref[part, :] = agb[j, :, state:]
 
     for d in range(1, nhead):
-        h_copy(d).wait_send()
+        for copy in h_copy(d):
+            copy.wait_send()
         a_copy(d, hd).wait_send()
-    rcopy(pass3, passr, psem, (), partner).wait_send()
-
-    @pl.loop(0, GROUP)
-    def _(k):
-        for copy in x_copy(k) + t_copy(k, True):
+
+    @pl.loop(0, GROUP)
+    def _(k):
+        for copy in x_copy(k) + t_copy(k):
             copy.wait_send()
         to_next, to_prev = z_copy(k)
 
         @pl.when(z < nz - 1)
         def _():
-            to_next.wait_send()
+            for copy in to_next:
+                copy.wait_send()
 
         @pl.when(z > 0)
         def _():
-            to_prev.wait_send()
+            for copy in to_prev:
+                copy.wait_send()
 
 
 def solution(mesh):
@@ -353,15 +398,20 @@
             + [vmem((blocks, hb, tok), F32)] * 2
             + [vmem((blocks, hb, state), F32)] * 4
             + [vmem((blocks,) + st, F32)] * 2
-            + [vmem((blocks, hb, state), F32)]
-            + [vmem((GROUP,) + st, F32)] * 8
+            + [vmem((GROUP,) + st, F32)] * 2
             + [vmem((blocks,) + st, F32)] * 2
-            + [vmem((nhead, piece, 2 * state), F32)] * 2
+            + [vmem((GROUP, 2) + st, jnp.int16)] * 4
+            + [vmem((GROUP, 3, hb, state), F32)] * 2
+            + [vmem((2, GROUP) + st, jnp.int16)] * 2
+            + [vmem((2, GROUP, hb, state), F32)] * 2
+            + [vmem((GROUP, 2, hb, state), F32)] * 2
+            + [vmem((nhead, piece, 2 * state), F32)]
+            + [vmem((nhead, piece, 2 * state), jnp.int16)] * 2
+            + [vmem((nhead, 8, 2 * state), F32)] * 2
             + [vmem((nhead, piece, 2 * state), BF16)]
             + [vmem((tok, 2 * state), F32)]
-            + [dma((2,))]
-            + [dma((2, 2, GROUP))] * 3
-            + [dma((2, nhead))] * 2
+            + [dma((2, 2, GROUP)), dma((2, 2, 2, GROUP)), dma((2, 2, GROUP))]
+            + [dma((2, 2, nhead)), dma((2, nhead))]
         )
         turned = jax.ShapeDtypeStruct((heads, width, tok), BF16)
         grads = jax.ShapeDtypeStruct((tok, state), BF16)
@@ -382,8 +432,8 @@
             step_raw.T,
             key_proj,
             query_proj,
-            jnp.broadcast_to(decay_log[:, None], (heads, state)),
-            jnp.broadcast_to(skip_gain[:, None], (heads, state)),
+            decay_log[None, :],
+            skip_gain[None, :],
         )
         return jnp.transpose(out, (2, 0, 1)), jnp.transpose(gs, (2, 0, 1)), gk, gq
 

time: 112 us -> 96.9 us (0.87)
  Pallas kernels: 103 us -> 90.1 us
  local copies, waits for them, and re-layouts: 8.58 us -> 5.92 us
    pallas_call x1, Pallas kernels: 103 us -> 90.1 us  [on_device(): pl.pallas_call(functools.partial(kernel, nseq, nhead), out_shape=(turned,...]
    broadcast_in_dim x2 -> x0, local copies, waits for them, and re-layouts: 2.66 us -> none  [the longest x1 1.33 us: on_device(): jnp.broadcast_to(decay_log[:, None], (heads, state))]
where the time goes in v2:
time: 96.9 us; the launch traced here: 96.7 us
  Pallas kernels  90.1 us (93%)
  local copies, waits for them, and re-layouts  5.92 us (6%)
    pallas_call x1, Pallas kernels, on_device(): pl.pallas_call(functools.partial(kernel, nseq, nhead), out_shape=(turned,...  90.1 us
    unnamed x10, local copies, waits for them, and re-layouts  5.92 us

profile of v2, /device:TPU:1, one launch (start us, length us, event | category | flops | bytes accessed | tf_op | source)
XLA Modules:
  0.0 96.7 jit_solution(13173610907110129179)
XLA Ops:
  0.6 90.1 %shard_map.111 = (bf16[32,64,512]{2,1,0:T(8,128)(2,1)}, bf16[32,64,512]{2,1,0:T(8,128)(2,1)}, bf16[512,128]{1,0:T(8,128)(2,1)}, bf16[512,128]{1,0:T(8,128)(2,1)}) custom-call(s32[6]{0:T(128)} %len_ref.1, bf16[32,64,512]{2,1,0:T(8,128)(2,1)} %bitcast.9, bf16[32,64,512]{2,1,0:T(8,128)(2,1)} %bitcast.10, bf16[32,512]{1,0:T(8,128)(2,1)} %bitcast.11, ...), custom_call_target="tpu_custom_call" | custom-call | tf_op jit(solution)/shard_map/pallas_call | solution.py:419
  90.8 0.0 copy-start
  90.8 3.3 %copy.16 = bf16[512,32,64]{0,2,1:T(8,128)(2,1)} copy(bf16[512,32,64]{0,2,1:T(8,128)(2,1)} %bitcast.8) | data formatting | bytes 4194304
  94.1 0.0 copy-done
  94.1 0.0 copy-start.2
  94.1 0.0 copy-start.1
  94.1 1.3 %copy.17 = bf16[512,32,64]{0,2,1:T(8,128)(2,1)} copy(bf16[512,32,64]{0,2,1:T(8,128)(2,1)S(1)} %bitcast.7) | data formatting | bytes 4194304
  95.4 0.0 copy-done.2
  95.4 0.7 copy.18
  96.1 0.0 copy-done.1
  96.1 0.7 copy.19
Async XLA Ops:
  90.8 3.3 %copy-start = (bf16[32,64,512]{2,1,0:T(8,128)(2,1)S(1)}, bf16[32,64,512]{2,1,0:T(8,128)(2,1)}, u32[]{:S(2)}) copy-start(bf16[32,64,512]{2,1,0:T(8,128)(2,1)} %get-tuple-element.9) | copy-start | bytes 6291460
  94.1 1.3 %copy-start.2 = (bf16[512,128]{1,0:T(8,128)(2,1)S(1)}, bf16[512,128]{1,0:T(8,128)(2,1)}, u32[]{:S(2)}) copy-start(bf16[512,128]{1,0:T(8,128)(2,1)} %get-tuple-element.18) | copy-start | bytes 393220
  94.1 2.0 %copy-start.1 = (bf16[512,128]{1,0:T(8,128)(2,1)S(1)}, bf16[512,128]{1,0:T(8,128)(2,1)}, u32[]{:S(2)}) copy-start(bf16[512,128]{1,0:T(8,128)(2,1)} %get-tuple-element.19) | copy-start | bytes 393220

commit v3 on v2

--- a/solution.py
+++ b/solution.py
@@ -216,57 +216,87 @@
             copy.wait_recv()
         into[k] = wide(zqr[way, k], zcr[way, k][:, None, :])
 
-    @pl.loop(0, GROUP)
-    def _(k):
-        p2(2 * k)
+    left = x == 0
+
+    def terms(k):
         b = x * GROUP + k
-        for copy in x_copy(k):
-            copy.wait_recv()
-        left = x == 0
         own, other = pass3[b][:, None, :], xsr[k, 2][:, None, :]
         s_in = wide(xqr[k, 0], xsr[k, 0][:, None, :])
         d_in = wide(xqr[k, 1], xsr[k, 1][:, None, :])
         pass0, pass1 = jnp.where(left, own, other), jnp.where(left, other, own)
         s0, s1 = jnp.where(left, sl[b], s_in), jnp.where(left, s_in, sl[b])
         d0, d1 = jnp.where(left, dlo[b], d_in), jnp.where(left, d_in, dlo[b])
-        both = pass0 * pass1
-        ps, pd = pass1 * s0 + s1, d0 + pass0 * d1
+        return pass0, pass1, s0, s1, d0, d1
+
+    @pl.loop(0, GROUP)
+    def _(k):
+        p2(2 * k)
+        for copy in x_copy(k):
+            copy.wait_recv()
+        pass0, pass1, s0, s1, d0, d1 = terms(k)
         to_next, to_prev = z_copy(k)
 
         @pl.when(first)
         def _():
-            zsr[k] = jnp.zeros_like(ps)
+            zsr[k] = jnp.zeros_like(s0)
 
         @pl.when(first & (nz > 1))
         def _():
-            z_send(0, k, ps, to_next)
+            z_send(0, k, pass1 * s0 + s1, to_next)
 
         @pl.when(last)
         def _():
-            zdr[k] = jnp.zeros_like(pd)
+            zdr[k] = jnp.zeros_like(d0)
 
         @pl.when(last & (nz > 1))
         def _():
-            z_send(1, k, pd, to_prev)
+            z_send(1, k, d0 + pass0 * d1, to_prev)
 
         p2(2 * k + 1)
 
+    inner = (z > 0) & (z < nz - 1)
+    low = z < nz // 2
+
+    def forward():
         @pl.when(z > 0)
         def _():
-            z_take(0, k, zsr, to_next)
-
-        @pl.when((z > 0) & (z < nz - 1))
-        def _():
-            z_send(0, k, both * zsr[k] + ps, to_next)
-
+            @pl.loop(0, GROUP)
+            def _(k):
+                to_next = z_copy(k)[0]
+                z_take(0, k, zsr, to_next)
+
+                @pl.when(inner)
+                def _():
+                    pass0, pass1, s0, s1, _, _ = terms(k)
+                    z_send(0, k, pass0 * pass1 * zsr[k] + pass1 * s0 + s1, to_next)
+
+    def backward():
         @pl.when(z < nz - 1)
         def _():
-            z_take(1, k, zdr, to_prev)
-
-        @pl.when((z > 0) & (z < nz - 1))
-        def _():
-            z_send(1, k, both * zdr[k] + pd, to_prev)
-
+            @pl.loop(0, GROUP)
+            def _(k):
+                to_prev = z_copy(k)[1]
+                z_take(1, k, zdr, to_prev)
+
+                @pl.when(inner)
+                def _():
+                    pass0, pass1, _, _, d0, d1 = terms(k)
+                    z_send(1, k, pass0 * pass1 * zdr[k] + d0 + pass0 * d1, to_prev)
+
+    @pl.when(low)
+    def _():
+        forward()
+
+    backward()
+
+    @pl.when(jnp.logical_not(low))
+    def _():
+        forward()
+
+    @pl.loop(0, GROUP)
+    def _(k):
+        b = x * GROUP + k
+        pass0, pass1, s0, _, _, d1 = terms(k)
         in0 = zsr[k]
         in1 = pass0 * in0 + s0
         gin1 = zdr[k]

time: 96.9 us -> 66.5 us (0.69)
  Pallas kernels: 90.1 us -> 59.8 us
    pallas_call x1, Pallas kernels: 90.1 us -> 59.8 us  [on_device(): pl.pallas_call(functools.partial(kernel, nseq, nhead), out_shape=(turned,...]
where the time goes in v3:
time: 66.5 us; the launch traced here: 66.3 us
  Pallas kernels  59.8 us (90%)
  local copies, waits for them, and re-layouts  5.92 us (9%)
    pallas_call x1, Pallas kernels, on_device(): pl.pallas_call(functools.partial(kernel, nseq, nhead), out_shape=(turned,...  59.8 us
    unnamed x10, local copies, waits for them, and re-layouts  5.92 us

profile of v3, /device:TPU:1, one launch (start us, length us, event | category | flops | bytes accessed | tf_op | source)
XLA Modules:
  0.0 66.3 jit_solution(3205422926523888686)
XLA Ops:
  0.6 59.8 %shard_map.111 = (bf16[32,64,512]{2,1,0:T(8,128)(2,1)}, bf16[32,64,512]{2,1,0:T(8,128)(2,1)}, bf16[512,128]{1,0:T(8,128)(2,1)}, bf16[512,128]{1,0:T(8,128)(2,1)}) custom-call(s32[6]{0:T(128)} %len_ref.1, bf16[32,64,512]{2,1,0:T(8,128)(2,1)} %bitcast.9, bf16[32,64,512]{2,1,0:T(8,128)(2,1)} %bitcast.10, bf16[32,512]{1,0:T(8,128)(2,1)} %bitcast.11, ...), custom_call_target="tpu_custom_call" | custom-call | tf_op jit(solution)/shard_map/pallas_call | solution.py:449
  60.4 0.0 copy-start
  60.4 3.3 %copy.16 = bf16[512,32,64]{0,2,1:T(8,128)(2,1)} copy(bf16[512,32,64]{0,2,1:T(8,128)(2,1)} %bitcast.8) | data formatting | bytes 4194304
  63.7 0.0 copy-done
  63.7 0.0 copy-start.2
  63.7 0.0 copy-start.1
  63.7 1.3 %copy.17 = bf16[512,32,64]{0,2,1:T(8,128)(2,1)} copy(bf16[512,32,64]{0,2,1:T(8,128)(2,1)S(1)} %bitcast.7) | data formatting | bytes 4194304
  65.0 0.0 copy-done.2
  65.0 0.7 copy.18
  65.7 0.0 copy-done.1
  65.7 0.7 copy.19
Async XLA Ops:
  60.4 3.3 %copy-start = (bf16[32,64,512]{2,1,0:T(8,128)(2,1)S(1)}, bf16[32,64,512]{2,1,0:T(8,128)(2,1)}, u32[]{:S(2)}) copy-start(bf16[32,64,512]{2,1,0:T(8,128)(2,1)} %get-tuple-element.9) | copy-start | bytes 6291460
  63.7 1.3 %copy-start.2 = (bf16[512,128]{1,0:T(8,128)(2,1)S(1)}, bf16[512,128]{1,0:T(8,128)(2,1)}, u32[]{:S(2)}) copy-start(bf16[512,128]{1,0:T(8,128)(2,1)} %get-tuple-element.18) | copy-start | bytes 393220
  63.7 2.0 %copy-start.1 = (bf16[512,128]{1,0:T(8,128)(2,1)S(1)}, bf16[512,128]{1,0:T(8,128)(2,1)}, u32[]{:S(2)}) copy-start(bf16[512,128]{1,0:T(8,128)(2,1)} %get-tuple-element.19) | copy-start | bytes 393220
